TPU v7x, 32 devices: a whole 2x2x4 slice. The times are simulated.
32 devices in a mesh: dp: 8 (over z, x), seq: 4 (over y, core).
Axes of the slice: x: 2, y: 2, z: 4, core: 2. Of those that a mesh axis runs over, the one named last changes fastest.
Arguments:
- tokens: bfloat16 [32, 6144], P('dp', 'seq'), may hold values from -6 to 6
- expert_ids: int32 [32, 2], P('dp'), may hold values from 0 to 7, all different within a row; in each aligned block of 4 rows (0 to 3, 4 to 7, ...) at most 2 rows name the same one
- router: bfloat16 [6144, 8], P('seq'), may hold values from -0.21875 to 0.21875
- w_gate: bfloat16 [5, 6144, 16384], P(None, 'seq', 'dp'), may hold values from -0.078125 to 0.078125
- w_up: bfloat16 [5, 6144, 16384], P(None, 'seq', 'dp'), may hold values from -0.078125 to 0.078125
- w_down: bfloat16 [5, 16384, 6144], P(None, 'dp', 'seq'), may hold values from -0.046875 to 0.046875
Outputs:
- mixed: bfloat16 [32, 6144], P('dp', 'seq')
Inputs may be any that keep to these rules, and one draw needn't show every extreme that they name: `expert_ids`: each row names 2 different experts. The 4 tokens of one index of dp name any expert at most 2 times, a bound that some block reaches.
All inputs are finite; a program needn't handle non-finite values.
Results may differ from a plain program's by a relative error of at most 0.0049.
Values may be sent and summed in bfloat16 or wider, within the bound.
No kernel may reach another device: no remote copies, remote signals or barrier semaphores. Data moves between devices by JAX's collectives and lax.ppermute only.
A program may use at most 192 MiB of HBM per device.

v0:
```python
import jax
import jax.numpy as jnp
from jax import lax
from jax.sharding import PartitionSpec as P

MOST = 2


def expert_rows(routes, expert, capacity):
    member = jnp.any(routes == expert, axis=1)
    position = jnp.cumsum(member.astype(jnp.int32)) - 1
    target = jnp.where(member, position, capacity)
    count_all = routes.shape[0]
    row_token = (
        jnp.zeros((capacity,), jnp.int32)
        .at[target]
        .set(jnp.arange(count_all, dtype=jnp.int32), mode="drop")
    )
    live_count = jnp.sum(member.astype(jnp.int32))
    return (row_token, jnp.maximum(position, 0), live_count)


def body(tokens, expert_ids, router, w_gate, w_up, w_down):
    gathered = lax.all_gather(tokens, "dp", axis=0, tiled=True)
    routes = lax.all_gather(expert_ids, "dp", axis=0, tiled=True)
    capacity = MOST * lax.axis_size("dp")
    block_rows = min(128, capacity)
    window_size = w_gate.shape[0]
    buffers = []
    positions = []
    live_blocks = []
    for expert in range(window_size):
        row_token, position, live_count = expert_rows(routes, expert, capacity)
        buffers.append(gathered[row_token])
        positions.append(position)
        live_blocks.append((live_count + block_rows - 1) // block_rows)
    gate_list = []
    up_list = []
    for expert in range(window_size):
        gate_part = jnp.dot(buffers[expert], w_gate[expert], preferred_element_type=jnp.float32)
        up_part = jnp.dot(buffers[expert], w_up[expert], preferred_element_type=jnp.float32)
        gate_list.append(gate_part)
        up_list.append(up_part)
    gate_parts = jnp.stack(gate_list)
    up_parts = jnp.stack(up_list)
    logit_part = jnp.dot(gathered, router, preferred_element_type=jnp.float32)
    gate_sum, up_sum, logits = lax.psum((gate_parts, up_parts, logit_part), "seq")
    hidden = (jax.nn.silu(gate_sum) * up_sum).astype(jnp.bfloat16)
    chosen = jnp.take_along_axis(logits, routes, axis=1)
    share_first = 1.0 / (1.0 + jnp.exp(chosen[:, 1] - chosen[:, 0]))
    share_second = 1.0 / (1.0 + jnp.exp(chosen[:, 0] - chosen[:, 1]))
    partial_value = jnp.zeros((gathered.shape[0], w_down.shape[2]), jnp.float32)
    for expert in range(window_size):
        expert_out = jnp.dot(hidden[expert], w_down[expert], preferred_element_type=jnp.float32)
        weighting = jnp.where(routes[:, 0] == expert, share_first, jnp.float32(0.0))
        weighting = weighting + jnp.where(routes[:, 1] == expert, share_second, jnp.float32(0.0))
        partial_value = partial_value + weighting[:, None] * expert_out[positions[expert]]
    return lax.psum_scatter(partial_value, "dp", scatter_dimension=0, tiled=True).astype(
        jnp.bfloat16
    )


def solution(mesh):
    placed = (
        P("dp", "seq"),
        P("dp", None),
        P("seq", None),
        P(None, "seq", "dp"),
        P(None, "seq", "dp"),
        P(None, "dp", "seq"),
    )
    return jax.shard_map(
        body, mesh=mesh, in_specs=placed, out_specs=P("dp", "seq"), check_vma=False
    )
```

profile of v0, /device:TPU:0, one launch (start us, length us, event | category | flops | bytes accessed | tf_op | source)
XLA Modules:
  0.0 207.5 jit_solution(11027577087069102119)
XLA Ops:
  6.5 22.7 %all-gather = s32[8,4,2]{1,2,0:T(2,128)S(1)} all-gather(s32[1,4,2]{1,2,0:T(2,128)} %bitcast.182), channel_id=1, replica_groups=mesh['dp'=8,'seq'=4] {'dp'}, dimensions={0}, use_global_device_ids=true | all-gather | bytes 288 | tf_op jit(solution)/shard_map/all_gather | solution.py:25
  29.3 0.1 copy.46
  29.4 0.1 copy.61
  29.5 0.1 copy.59
  29.6 0.1 copy.57
  29.7 0.1 copy.63
  29.8 0.1 compare_reduce_fusion
  30.0 0.1 copy.55
  30.1 0.1 copy.54
  30.2 0.1 maximum_reduce_fusion.4
  30.3 0.7 scatter_custom_fusion
  31.0 0.1 copy.60
  31.2 0.1 maximum_reduce_fusion.1
  31.3 0.7 scatter_custom_fusion.3
  32.0 0.1 copy.58
  32.1 0.1 maximum_reduce_fusion.2
  32.3 0.7 scatter_custom_fusion.2
  33.0 0.1 copy.56
  33.1 0.1 maximum_reduce_fusion.3
  33.2 0.7 scatter_custom_fusion.1
  33.9 0.1 copy.62
  34.1 0.1 maximum_reduce_fusion
  34.2 0.7 scatter_custom_fusion.4
  34.9 30.8 %all-gather.1 = bf16[8,4,1536]{2,1,0:T(4,128)(2,1)S(1)} all-gather(bf16[1,4,1536]{2,1,0:T(4,128)(2,1)} %bitcast.176), channel_id=1, replica_groups=mesh['dp'=8,'seq'=4] {'dp'}, dimensions={0}, use_global_device_ids=true | all-gather | bytes 110592 | tf_op jit(solution)/shard_map/all_gather | solution.py:24
  65.7 0.6 gather_fusion.4
  66.3 0.6 gather_fusion.3
  66.9 0.6 gather_fusion.2
  67.5 0.6 gather_fusion.1
  68.1 0.6 gather_fusion
  68.7 3.9 %fusion.48 = f32[5,16,2048]{2,1,0:T(8,128)S(1)} fusion(bf16[16,1536]{1,0:T(8,128)(2,1)S(1)} %gather_fusion, bf16[5,1536,2048]{2,1,0:T(8,128)(2,1)} %param.9), kind=kOutput, calls=%fused_computation.62 | convolution fusion | flops 100663296 | bytes 6471680 | tf_op jit(solution)/shard_map/dot_general | solution.py:40
  72.6 4.4 %fusion.78 = f32[5,16,2048]{2,1,0:T(8,128)S(1)} fusion(bf16[16,1536]{1,0:T(8,128)(2,1)S(1)} %gather_fusion, bf16[5,1536,2048]{2,1,0:T(8,128)(2,1)} %param.10), kind=kOutput, calls=%fused_computation.72 | convolution fusion | flops 100663296 | bytes 6471680 | tf_op jit(solution)/shard_map/dot_general | solution.py:41
  77.0 4.5 %fusion.54 = f32[5,16,2048]{2,1,0:T(8,128)S(1)} fusion(f32[5,16,2048]{2,1,0:T(8,128)S(1)} %fusion.48, bf16[16,1536]{1,0:T(8,128)(2,1)S(1)} %gather_fusion.1, bf16[5,1536,2048]{2,1,0:T(8,128)(2,1)} %param.9), kind=kOutput, calls=%fused_computation.64 | convolution fusion | flops 100663296 | bytes 6471680 | tf_op jit(solution)/shard_map/dot_general | solution.py:40
  81.4 4.5 %fusion.84 = f32[5,16,2048]{2,1,0:T(8,128)S(1)} fusion(f32[5,16,2048]{2,1,0:T(8,128)S(1)} %fusion.78, bf16[16,1536]{1,0:T(8,128)(2,1)S(1)} %gather_fusion.1, bf16[5,1536,2048]{2,1,0:T(8,128)(2,1)} %param.10), kind=kOutput, calls=%fused_computation.74 | convolution fusion | flops 100663296 | bytes 6471680 | tf_op jit(solution)/shard_map/dot_general | solution.py:41
  85.9 3.7 %fusion.60 = f32[5,16,2048]{2,1,0:T(8,128)S(1)} fusion(f32[5,16,2048]{2,1,0:T(8,128)S(1)} %fusion.54, bf16[16,1536]{1,0:T(8,128)(2,1)S(1)} %gather_fusion.2, bf16[5,1536,2048]{2,1,0:T(8,128)(2,1)} %param.9), kind=kOutput, calls=%fused_computation.66 | convolution fusion | flops 100663296 | bytes 6471680 | tf_op jit(solution)/shard_map/dot_general | solution.py:40
  89.6 0.9 fusion.90
  90.6 3.7 %fusion.66 = f32[5,16,2048]{2,1,0:T(8,128)S(1)} fusion(f32[5,16,2048]{2,1,0:T(8,128)S(1)} %fusion.60, bf16[16,1536]{1,0:T(8,128)(2,1)S(1)} %gather_fusion.3, bf16[5,1536,2048]{2,1,0:T(8,128)(2,1)} %param.9), kind=kOutput, calls=%fused_computation.68 | convolution fusion | flops 100663296 | bytes 6471680 | tf_op jit(solution)/shard_map/dot_general | solution.py:40
  94.3 0.9 fusion.96
  95.2 3.7 %fusion.72 = f32[5,16,2048]{2,1,0:T(8,128)S(1)} fusion(f32[5,16,2048]{2,1,0:T(8,128)S(1)} %fusion.66, bf16[16,1536]{1,0:T(8,128)(2,1)S(1)} %gather_fusion.4, bf16[5,1536,2048]{2,1,0:T(8,128)(2,1)} %param.9), kind=kOutput, calls=%fused_computation.70 | convolution fusion | flops 100663296 | bytes 6471680 | tf_op jit(solution)/shard_map/dot_general | solution.py:40
  99.0 0.9 fusion.102
  99.9 0.9 copy-done.2
  100.9 0.1 copy.51
  101.0 0.1 reshape.260
  101.1 0.1 fusion.120
  101.2 5.7 %psum.21 = f32[32,8]{0,1:T(8,128)S(1)} all-reduce(f32[32,8]{0,1:T(8,128)S(1)} %fusion.120), channel_id=1, replica_groups=mesh['dp'=8,'seq'=4] {'seq'}, use_global_device_ids=true, to_apply=%region_0.0 | all-reduce | flops 256 | bytes 2048 | tf_op jit(solution)/shard_map/psum | solution.py:47
  106.9 0.7 gather_fusion.10
  107.6 0.1 reshape.263
  107.8 0.6 dynamic-slice
  109.1 0.1 add_divide_fusion.1
  109.2 0.3 add_reduce_fusion.4
  109.4 28.0 %all-reduce.5.cloned.1.call-done = (f32[5,16,2048]{2,1,0:T(8,128)}, f32[5,16,2048]{2,1,0:T(8,128)}) async-done(((f32[5,16,2048]{2,1,0:T(8,128)}, f32[5,16,2048]{2,1,0:T(8,128)}), (f32[5,16,2048]{2,1,0:T(8,128)}, f32[5,16,2048]{2,1,0:T(8,128)})) %all-reduce.5.cloned.1.call-update) | async-done | bytes 1310736 | tf_op jit(solution)/shard_map/psum | solution.py:47
  137.4 1.5 multiply_convert_fusion
  138.9 3.7 %fusion = f32[16,1536]{1,0:T(8,128)S(1)} fusion(bf16[5,2048,1536]{2,1,0:T(8,128)(2,1)} %param.11, bf16[5,16,2048]{2,1,0:T(8,128)(2,1)S(1)} %multiply_convert_fusion), kind=kOutput, calls=%fused_computation.16 | convolution fusion | flops 100663296 | bytes 6455296 | tf_op jit(solution)/shard_map/dot_general | solution.py:54
  142.6 3.7 %fusion.2 = f32[16,1536]{1,0:T(8,128)S(1)} fusion(bf16[5,2048,1536]{2,1,0:T(8,128)(2,1)} %param.11, bf16[5,16,2048]{2,1,0:T(8,128)(2,1)S(1)} %multiply_convert_fusion), kind=kOutput, calls=%fused_computation.18 | convolution fusion | flops 100663296 | bytes 6455296 | tf_op jit(solution)/shard_map/dot_general | solution.py:54
  146.3 3.7 %fusion.4 = f32[16,1536]{1,0:T(8,128)S(1)} fusion(bf16[5,2048,1536]{2,1,0:T(8,128)(2,1)} %param.11, bf16[5,16,2048]{2,1,0:T(8,128)(2,1)S(1)} %multiply_convert_fusion), kind=kOutput, calls=%fused_computation.20 | convolution fusion | flops 100663296 | bytes 6455296 | tf_op jit(solution)/shard_map/dot_general | solution.py:54
  150.0 3.7 %fusion.6 = f32[16,1536]{1,0:T(8,128)S(1)} fusion(bf16[5,2048,1536]{2,1,0:T(8,128)(2,1)} %param.11, bf16[5,16,2048]{2,1,0:T(8,128)(2,1)S(1)} %multiply_convert_fusion), kind=kOutput, calls=%fused_computation.22 | convolution fusion | flops 100663296 | bytes 6455296 | tf_op jit(solution)/shard_map/dot_general | solution.py:54
  153.7 3.7 %fusion.8 = f32[16,1536]{1,0:T(8,128)S(1)} fusion(bf16[5,2048,1536]{2,1,0:T(8,128)(2,1)} %param.11, bf16[5,16,2048]{2,1,0:T(8,128)(2,1)S(1)} %multiply_convert_fusion), kind=kOutput, calls=%fused_computation.24 | convolution fusion | flops 100663296 | bytes 6455296 | tf_op jit(solution)/shard_map/dot_general | solution.py:54
  157.4 0.6 gather_fusion.9
  158.1 0.6 gather_fusion.8
  158.7 0.6 gather_fusion.7
  159.3 0.6 gather_fusion.5
  160.0 0.6 gather_fusion.6
  160.6 0.1 multiply_add_fusion
  160.8 39.3 %all-reduce.6 = bf16[32,1536]{1,0:T(8,128)(2,1)S(1)} all-reduce(f32[32,1536]{1,0:T(8,128)S(1)} %multiply_add_fusion), channel_id=2, replica_groups=mesh['dp'=8,'seq'=4] {'dp'}, use_global_device_ids=true, to_apply=%region_18.19.clone | all-reduce | flops 49152 | bytes 294912
  200.0 0.6 dynamic-slice_convert_fusion
  (45 shorter events, 0.6 us)
Async XLA Ops:
  6.5 94.6 %copy-start = (bf16[1536,8]{0,1:T(8,128)(2,1)S(1)}, bf16[1536,8]{0,1:T(8,128)(2,1)}, u32[]{:S(2)}) copy-start(bf16[1536,8]{0,1:T(8,128)(2,1)} %param.8) | copy-start | bytes 73732
  6.5 130.9 %all-reduce.5.cloned.1.call-start = ((), (), s32[]{:S(2)}) async-start(), calls=%async_computation | async-start | bytes 2621440 | tf_op jit(solution)/shard_map/psum | solution.py:47
  68.7 20.9 %copy-start.1 = (bf16[5,1536,2048]{2,1,0:T(8,128)(2,1)S(1)}, bf16[5,1536,2048]{2,1,0:T(8,128)(2,1)}, u32[]{:S(2)}) copy-start(bf16[5,1536,2048]{2,1,0:T(8,128)(2,1)} %param.10) | copy-start | bytes 94371840
  81.4 26.3 %copy-start.4 = (u32[32]{0:T(128)S(1)}, u32[32]{0:T(128)}, u32[]{:S(2)}) copy-start(u32[32]{0:T(128)} %constant.79) | copy-start | bytes 388
  99.0 0.9 copy-start.3
  99.9 0.9 copy-start.2
Sparse Core Ops, SparseCore 0:
  100.9 36.4 all-reduce.4
where the time goes:
time: 208 us; the launch traced here: 207 us
  blocking collectives  98.3 us (47%)
  matrix products  49.9 us (24%)
  waiting for transfers between devices  28 us (13%)
  between operations  14.4 us (7%)
  local copies, waits for them, and re-layouts  13.9 us (7%)
  other arithmetic  3.05 us (1%)
    unnamed x1, blocking collectives  39.3 us
    all_gather x1, blocking collectives, body(): gathered = lax.all_gather(tokens, 'dp', axis=0, tiled=True)  30.8 us
    psum x1, waiting for transfers between devices, body(): lax.psum((gate_parts, up_parts, logit_part), 'seq')  28 us
    all_gather x1, blocking collectives, body(): routes = lax.all_gather(expert_ids, 'dp', axis=0, tiled=True)  22.7 us
    dot_general x5, matrix products, body(): jnp.dot(buffers[expert], w_gate[expert], preferred_element_type=jnp.float32)  19.5 us
    dot_general x5, matrix products, body(): jnp.dot(hidden[expert], w_down[expert], preferred_element_type=jnp.float32)  18.6 us
    dot_general x5, matrix products, body(): jnp.dot(buffers[expert], w_up[expert], preferred_element_type=jnp.float32)  11.6 us
    psum x1, blocking collectives, body(): lax.psum((gate_parts, up_parts, logit_part), 'seq')  5.66 us
  transfers between devices with their start and end apart: 1, of which 1 were waited for; matrix products, arithmetic and copies ran while one was open for 1% of the time, Pallas kernels for 0%

commit v1 on v0

--- a/solution.py
+++ b/solution.py
@@ -4,6 +4,18 @@
 from jax.sharding import PartitionSpec as P
 
 MOST = 2
+
+
+def gather_by_bits(x, axis, dim):
+    ways, here = (lax.axis_size(axis), lax.axis_index(axis))
+    grown, reach = (x, 1)
+    while reach < ways:
+        theirs = lax.ppermute(grown, axis, [(d, d ^ reach) for d in range(ways)])
+        mine_first = jnp.concatenate([grown, theirs], axis=dim)
+        theirs_first = jnp.concatenate([theirs, grown], axis=dim)
+        grown = jnp.where(here & reach == 0, mine_first, theirs_first)
+        reach = 2 * reach
+    return grown
 
 
 def expert_rows(routes, expert, capacity):
@@ -21,7 +33,7 @@
 
 
 def body(tokens, expert_ids, router, w_gate, w_up, w_down):
-    gathered = lax.all_gather(tokens, "dp", axis=0, tiled=True)
+    gathered = gather_by_bits(tokens, "dp", 0)
     routes = lax.all_gather(expert_ids, "dp", axis=0, tiled=True)
     capacity = MOST * lax.axis_size("dp")
     block_rows = min(128, capacity)

time: 208 us -> 188 us (0.904)
  blocking collectives: 98.3 us -> 65 us
  waiting for transfers between devices: 28 us -> 36.3 us
  starting transfers between devices: 0.01 us -> 3.11 us
    all_gather x1 -> x0, blocking collectives: 30.8 us -> none  [body(): gathered = lax.all_gather(tokens, 'dp', axis=0, tiled=True)]
    ppermute x0 -> x3, waiting for transfers between devices: none -> 6.65 us  [gather_by_bits(): theirs = lax.ppermute(grown, axis, [(d, d ^ reach) for d in range(ways)])]
    ppermute x0 -> x3, starting transfers between devices: none -> 3.11 us  [gather_by_bits(): theirs = lax.ppermute(grown, axis, [(d, d ^ reach) for d in range(ways)])]
    all_gather x1, blocking collectives: 22.7 us -> 20.1 us  [body(): routes = lax.all_gather(expert_ids, 'dp', axis=0, tiled=True)]
  transfers between devices with their start and end apart: 1 -> 4, of which waited for: 1 -> 3; matrix products, arithmetic and copies ran while one was open for 1% -> 5% of each run, Pallas kernels for 0% -> 0%
where the time goes in v1:
time: 188 us; the launch traced here: 187 us
  blocking collectives  65 us (35%)
  matrix products  49.9 us (27%)
  waiting for transfers between devices  36.3 us (19%)
  local copies, waits for them, and re-layouts  14.5 us (8%)
  between operations  14.4 us (8%)
  other arithmetic  3.9 us (2%)
  starting transfers between devices  3.11 us (2%)
    unnamed x1, blocking collectives  39.3 us
    psum x1, waiting for transfers between devices, body(): lax.psum((gate_parts, up_parts, logit_part), 'seq')  29.6 us
    all_gather x1, blocking collectives, body(): routes = lax.all_gather(expert_ids, 'dp', axis=0, tiled=True)  20.1 us
    dot_general x5, matrix products, body(): jnp.dot(buffers[expert], w_gate[expert], preferred_element_type=jnp.float32)  19.5 us
    dot_general x5, matrix products, body(): jnp.dot(hidden[expert], w_down[expert], preferred_element_type=jnp.float32)  18.6 us
    dot_general x5, matrix products, body(): jnp.dot(buffers[expert], w_up[expert], preferred_element_type=jnp.float32)  11.6 us
    ppermute x3, waiting for transfers between devices, gather_by_bits(): theirs = lax.ppermute(grown, axis, [(d, d ^ reach) for d in range(ways)])  6.65 us
    psum x1, blocking collectives, body(): lax.psum((gate_parts, up_parts, logit_part), 'seq')  5.65 us
  transfers between devices with their start and end apart: 4, of which 3 were waited for; matrix products, arithmetic and copies ran while one was open for 5% of the time, Pallas kernels for 0%

profile of v1, /device:TPU:0, one launch (start us, length us, event | category | flops | bytes accessed | tf_op | source)
XLA Modules:
  0.0 187.1 jit_solution(5458492290385381992)
XLA Ops:
  6.5 3.0 %collective-permute-start = (bf16[4,1536]{1,0:T(4,128)(2,1)}, bf16[4,1536]{1,0:T(4,128)(2,1)S(1)}, u32[]{:S(2)}, u32[]{:S(2)}) collective-permute-start(bf16[4,1536]{1,0:T(4,128)(2,1)} %param.6), channel_id=1, source_target_pairs={{0,4},{4,0},{8,12},{12,8},{16,20},{20,16},{24,28},{28,24},{1,5},{5... | collective-permute-start | bytes 36872 | tf_op jit(solution)/shard_map/ppermute | solution.py:13
  9.5 20.1 %all-gather = s32[8,4,2]{1,2,0:T(2,128)S(1)} all-gather(s32[1,4,2]{1,2,0:T(2,128)} %bitcast.180), channel_id=1, replica_groups=mesh['dp'=8,'seq'=4] {'dp'}, dimensions={0}, use_global_device_ids=true | all-gather | bytes 288 | tf_op jit(solution)/shard_map/all_gather | solution.py:37
  29.8 0.1 compare_reduce_fusion
  30.0 0.1 copy.61
  30.1 0.1 copy.59
  30.2 0.1 copy.57
  30.3 0.1 copy.63
  30.4 0.1 copy.55
  30.6 0.1 maximum_reduce_fusion.4
  30.8 0.7 scatter_custom_fusion
  31.5 0.1 copy.60
  31.6 0.1 maximum_reduce_fusion.1
  31.7 0.7 scatter_custom_fusion.3
  32.4 0.1 copy.58
  32.6 0.1 maximum_reduce_fusion.2
  32.7 0.7 scatter_custom_fusion.2
  33.4 0.1 copy.56
  33.5 0.1 maximum_reduce_fusion.3
  33.7 0.7 scatter_custom_fusion.1
  34.3 0.1 copy.62
  34.5 0.1 maximum_reduce_fusion
  34.6 0.7 scatter_custom_fusion.4
  35.5 0.8 maximum_select_fusion.2
  36.4 3.8 %collective-permute-done.1 = bf16[8,1536]{1,0:T(8,128)(2,1)S(1)} collective-permute-done((bf16[8,1536]{1,0:T(8,128)(2,1)S(1)}, bf16[8,1536]{1,0:T(8,128)(2,1)S(1)}, u32[]{:S(2)}, u32[]{:S(2)}) %collective-permute-start.1) | collective-permute-done | bytes 24608 | tf_op jit(solution)/shard_map/ppermute | solution.py:13
  40.3 0.1 copy.51
  40.4 0.1 reshape.260
  40.5 1.2 dynamic-slice
  42.4 2.9 %collective-permute-done.2 = bf16[16,1536]{1,0:T(8,128)(2,1)S(1)} collective-permute-done((bf16[16,1536]{1,0:T(8,128)(2,1)S(1)}, bf16[16,1536]{1,0:T(8,128)(2,1)S(1)}, u32[]{:S(2)}, u32[]{:S(2)}) %collective-permute-start.2) | collective-permute-done | bytes 49184 | tf_op jit(solution)/shard_map/ppermute | solution.py:13
  45.3 0.6 gather_fusion.4
  45.9 0.6 gather_fusion.3
  46.5 0.6 gather_fusion.2
  47.1 0.6 gather_fusion.1
  47.7 0.6 gather_fusion
  48.3 3.9 %fusion.48 = f32[5,16,2048]{2,1,0:T(8,128)S(1)} fusion(bf16[16,1536]{1,0:T(8,128)(2,1)S(1)} %gather_fusion, bf16[5,1536,2048]{2,1,0:T(8,128)(2,1)} %param.9), kind=kOutput, calls=%fused_computation.62 | convolution fusion | flops 100663296 | bytes 6471680 | tf_op jit(solution)/shard_map/dot_general | solution.py:52
  52.1 4.4 %fusion.78 = f32[5,16,2048]{2,1,0:T(8,128)S(1)} fusion(bf16[16,1536]{1,0:T(8,128)(2,1)S(1)} %gather_fusion, bf16[5,1536,2048]{2,1,0:T(8,128)(2,1)} %param.10), kind=kOutput, calls=%fused_computation.72 | convolution fusion | flops 100663296 | bytes 6471680 | tf_op jit(solution)/shard_map/dot_general | solution.py:53
  56.5 4.5 %fusion.54 = f32[5,16,2048]{2,1,0:T(8,128)S(1)} fusion(f32[5,16,2048]{2,1,0:T(8,128)S(1)} %fusion.48, bf16[16,1536]{1,0:T(8,128)(2,1)S(1)} %gather_fusion.1, bf16[5,1536,2048]{2,1,0:T(8,128)(2,1)} %param.9), kind=kOutput, calls=%fused_computation.64 | convolution fusion | flops 100663296 | bytes 6471680 | tf_op jit(solution)/shard_map/dot_general | solution.py:52
  61.0 4.5 %fusion.84 = f32[5,16,2048]{2,1,0:T(8,128)S(1)} fusion(f32[5,16,2048]{2,1,0:T(8,128)S(1)} %fusion.78, bf16[16,1536]{1,0:T(8,128)(2,1)S(1)} %gather_fusion.1, bf16[5,1536,2048]{2,1,0:T(8,128)(2,1)} %param.10), kind=kOutput, calls=%fused_computation.74 | convolution fusion | flops 100663296 | bytes 6471680 | tf_op jit(solution)/shard_map/dot_general | solution.py:53
  65.5 3.7 %fusion.60 = f32[5,16,2048]{2,1,0:T(8,128)S(1)} fusion(f32[5,16,2048]{2,1,0:T(8,128)S(1)} %fusion.54, bf16[16,1536]{1,0:T(8,128)(2,1)S(1)} %gather_fusion.2, bf16[5,1536,2048]{2,1,0:T(8,128)(2,1)} %param.9), kind=kOutput, calls=%fused_computation.66 | convolution fusion | flops 100663296 | bytes 6471680 | tf_op jit(solution)/shard_map/dot_general | solution.py:52
  69.2 0.9 fusion.90
  70.1 3.7 %fusion.66 = f32[5,16,2048]{2,1,0:T(8,128)S(1)} fusion(f32[5,16,2048]{2,1,0:T(8,128)S(1)} %fusion.60, bf16[16,1536]{1,0:T(8,128)(2,1)S(1)} %gather_fusion.3, bf16[5,1536,2048]{2,1,0:T(8,128)(2,1)} %param.9), kind=kOutput, calls=%fused_computation.68 | convolution fusion | flops 100663296 | bytes 6471680 | tf_op jit(solution)/shard_map/dot_general | solution.py:52
  73.9 0.9 fusion.96
  74.8 3.7 %fusion.72 = f32[5,16,2048]{2,1,0:T(8,128)S(1)} fusion(f32[5,16,2048]{2,1,0:T(8,128)S(1)} %fusion.66, bf16[16,1536]{1,0:T(8,128)(2,1)S(1)} %gather_fusion.4, bf16[5,1536,2048]{2,1,0:T(8,128)(2,1)} %param.9), kind=kOutput, calls=%fused_computation.70 | convolution fusion | flops 100663296 | bytes 6471680 | tf_op jit(solution)/shard_map/dot_general | solution.py:52
  78.5 0.9 fusion.102
  79.5 0.9 copy-done.2
  80.4 0.1 fusion.120
  80.5 5.6 %psum.21 = f32[32,8]{0,1:T(8,128)S(1)} all-reduce(f32[32,8]{0,1:T(8,128)S(1)} %fusion.120), channel_id=1, replica_groups=mesh['dp'=8,'seq'=4] {'seq'}, use_global_device_ids=true, to_apply=%region_0.1 | all-reduce | flops 256 | bytes 2048 | tf_op jit(solution)/shard_map/psum | solution.py:59
  86.1 0.7 gather_fusion.10
  86.9 0.1 reshape.263
  87.1 0.3 add_reduce_fusion.4
  87.3 29.6 %all-reduce.5.cloned.1.call-done = (f32[5,16,2048]{2,1,0:T(8,128)}, f32[5,16,2048]{2,1,0:T(8,128)}) async-done(((f32[5,16,2048]{2,1,0:T(8,128)}, f32[5,16,2048]{2,1,0:T(8,128)}), (f32[5,16,2048]{2,1,0:T(8,128)}, f32[5,16,2048]{2,1,0:T(8,128)})) %all-reduce.5.cloned.1.call-update) | async-done | bytes 1310736 | tf_op jit(solution)/shard_map/psum | solution.py:59
  117.0 1.5 multiply_convert_fusion
  118.4 3.7 %fusion = f32[16,1536]{1,0:T(8,128)S(1)} fusion(bf16[5,2048,1536]{2,1,0:T(8,128)(2,1)} %param.11, bf16[5,16,2048]{2,1,0:T(8,128)(2,1)S(1)} %multiply_convert_fusion), kind=kOutput, calls=%fused_computation.16 | convolution fusion | flops 100663296 | bytes 6455296 | tf_op jit(solution)/shard_map/dot_general | solution.py:66
  122.1 3.7 %fusion.2 = f32[16,1536]{1,0:T(8,128)S(1)} fusion(bf16[5,2048,1536]{2,1,0:T(8,128)(2,1)} %param.11, bf16[5,16,2048]{2,1,0:T(8,128)(2,1)S(1)} %multiply_convert_fusion), kind=kOutput, calls=%fused_computation.18 | convolution fusion | flops 100663296 | bytes 6455296 | tf_op jit(solution)/shard_map/dot_general | solution.py:66
  125.8 3.7 %fusion.4 = f32[16,1536]{1,0:T(8,128)S(1)} fusion(bf16[5,2048,1536]{2,1,0:T(8,128)(2,1)} %param.11, bf16[5,16,2048]{2,1,0:T(8,128)(2,1)S(1)} %multiply_convert_fusion), kind=kOutput, calls=%fused_computation.20 | convolution fusion | flops 100663296 | bytes 6455296 | tf_op jit(solution)/shard_map/dot_general | solution.py:66
  129.6 3.7 %fusion.6 = f32[16,1536]{1,0:T(8,128)S(1)} fusion(bf16[5,2048,1536]{2,1,0:T(8,128)(2,1)} %param.11, bf16[5,16,2048]{2,1,0:T(8,128)(2,1)S(1)} %multiply_convert_fusion), kind=kOutput, calls=%fused_computation.22 | convolution fusion | flops 100663296 | bytes 6455296 | tf_op jit(solution)/shard_map/dot_general | solution.py:66
  133.3 3.7 %fusion.8 = f32[16,1536]{1,0:T(8,128)S(1)} fusion(bf16[5,2048,1536]{2,1,0:T(8,128)(2,1)} %param.11, bf16[5,16,2048]{2,1,0:T(8,128)(2,1)S(1)} %multiply_convert_fusion), kind=kOutput, calls=%fused_computation.24 | convolution fusion | flops 100663296 | bytes 6455296 | tf_op jit(solution)/shard_map/dot_general | solution.py:66
  137.0 0.6 gather_fusion.9
  137.6 0.6 gather_fusion.8
  138.3 0.6 gather_fusion.7
  138.9 0.6 gather_fusion.5
  139.5 0.6 gather_fusion.6
  140.2 0.1 multiply_add_fusion
  140.3 39.3 %all-reduce.6 = bf16[32,1536]{1,0:T(8,128)(2,1)S(1)} all-reduce(f32[32,1536]{1,0:T(8,128)S(1)} %multiply_add_fusion), channel_id=2, replica_groups=mesh['dp'=8,'seq'=4] {'dp'}, use_global_device_ids=true, to_apply=%region_18.19.clone | all-reduce | flops 49152 | bytes 294912
  179.6 0.6 dynamic-slice_convert_fusion
  (50 shorter events, 1.0 us)
Async XLA Ops:
  6.5 73.8 %copy-start = (bf16[1536,8]{0,1:T(8,128)(2,1)S(1)}, bf16[1536,8]{0,1:T(8,128)(2,1)}, u32[]{:S(2)}) copy-start(bf16[1536,8]{0,1:T(8,128)(2,1)} %param.8) | copy-start | bytes 73732
  6.5 110.4 %all-reduce.5.cloned.1.call-start = ((), (), s32[]{:S(2)}) async-start(), calls=%async_computation | async-start | bytes 2621440 | tf_op jit(solution)/shard_map/psum | solution.py:59
  6.5 28.9 %collective-permute-start = (bf16[4,1536]{1,0:T(4,128)(2,1)}, bf16[4,1536]{1,0:T(4,128)(2,1)S(1)}, u32[]{:S(2)}, u32[]{:S(2)}) collective-permute-start(bf16[4,1536]{1,0:T(4,128)(2,1)} %param.6), channel_id=1, source_target_pairs={{0,4},{4,0},{8,12},{12,8},{16,20},{20,16},{24,28},{28,24},{1,5},{5... | collective-permute-start | bytes 36872 | tf_op jit(solution)/shard_map/ppermute | solution.py:13
  36.3 3.9 %collective-permute-start.1 = (bf16[8,1536]{1,0:T(8,128)(2,1)S(1)}, bf16[8,1536]{1,0:T(8,128)(2,1)S(1)}, u32[]{:S(2)}, u32[]{:S(2)}) collective-permute-start(bf16[8,1536]{1,0:T(8,128)(2,1)S(1)} %maximum_select_fusion.2), channel_id=1, source_target_pairs={{0,8},{4,12},{8,0},{12,4},{16,24},{20,28},{24,16},{28,20},{1,9},{5... | collective-permute-start | bytes 73736 | tf_op jit(solution)/shard_map/ppermute | solution.py:13
  40.2 5.1 %collective-permute-start.2 = (bf16[16,1536]{1,0:T(8,128)(2,1)S(1)}, bf16[16,1536]{1,0:T(8,128)(2,1)S(1)}, u32[]{:S(2)}, u32[]{:S(2)}) collective-permute-start(bf16[16,1536]{1,0:T(8,128)(2,1)S(1)} %maximum_select_fusion.1), channel_id=1, source_target_pairs={{0,16},{4,20},{8,24},{12,28},{16,0},{20,4},{24,8},{28,12},{1,17},{... | collective-permute-start | bytes 147464 | tf_op jit(solution)/shard_map/ppermute | solution.py:13
  48.3 20.9 %copy-start.1 = (bf16[5,1536,2048]{2,1,0:T(8,128)(2,1)S(1)}, bf16[5,1536,2048]{2,1,0:T(8,128)(2,1)}, u32[]{:S(2)}) copy-start(bf16[5,1536,2048]{2,1,0:T(8,128)(2,1)} %param.10) | copy-start | bytes 94371840
  78.5 0.9 copy-start.3
  79.5 0.9 copy-start.2
Sparse Core Ops, SparseCore 0:
  80.5 36.4 all-reduce.4
